TPU v7x, 32 devices: a whole 2x2x4 slice. The times are simulated.
32 devices in a mesh: member: 4 (over z), space: 8 (over y, x, core).
Axes of the slice: x: 2, y: 2, z: 4, core: 2. Of those that a mesh axis runs over, the one named last changes fastest.
Arguments:
- particles: float32 [32, 2, 200, 800], P('member', None, 'space'), may hold values from -8 to 8
- loglik_grad: float32 [32, 2, 200, 800], P('member', None, 'space'), may hold values from -0.00036621094 to 0.00036621094
- wave_prev: float32 [32, 2, 200, 800], P('member', None, 'space'), may hold values from -6 to 6
- wave_now: float32 [32, 2, 200, 800], P('member', None, 'space'), may hold values from -6 to 6
- ghosts: float32 [32, 8, 200, 800], P('member', None, 'space'), may hold values from -6 to 6
- src_cell: int32 [32], P('member'), may hold values from 0 to 159999
Outputs:
- new_particles: float32 [32, 2, 200, 800], P('member', None, 'space')
- wave_before: float32 [32, 2, 200, 800], P('member', None, 'space')
- wave_after: float32 [32, 2, 200, 800], P('member', None, 'space')
Inputs may be any that keep to these rules, and one draw needn't show every extreme that they name: `src_cell`: the flat index 800 * x + y of each particle's source cell on depth plane 0.
All inputs are finite; a program needn't handle non-finite values.
Results may differ from a plain program's by a relative error of at most 0.0003.
Values sent between devices are 32-bit elements; how exact they have to be, the bound alone decides.
No kernel may reach another device: no remote copies, remote signals or barrier semaphores. Data moves between devices by JAX's collectives and lax.ppermute only.
A program may use at most 128 MiB of HBM per device.

v0:
```python
import math

import jax
import jax.numpy as jnp
from jax import lax
from jax.sharding import PartitionSpec as P

GHOST = 4
STEPS = 4


weights = (-205.0 / 72.0, 8.0 / 5.0, -1.0 / 5.0, 8.0 / 315.0, -1.0 / 560.0)
step_size = 0.25
courant = 0.3


def extended(cells, sides, width):
    for axis, dim in sides:
        count = lax.axis_size(axis)
        ends = count - 1
        head = lax.slice_in_dim(cells, 0, width, axis=dim)
        tail = lax.slice_in_dim(cells, cells.shape[dim] - width, cells.shape[dim], axis=dim)
        cells = jnp.concatenate(
            [
                lax.ppermute(tail, axis, [(i, (i + 1) % count) for i in range(ends)]),
                cells,
                lax.ppermute(head, axis, [((i + 1) % count, i) for i in range(ends)]),
            ],
            axis=dim,
        )
    return cells


def laplace(wide, top, bottom):
    extent = wide.shape[-2] - 8
    center = wide[..., 4 : 4 + extent, :]
    depth = center.shape[-3]
    across = center.shape[-1]
    pad_spec = [(0, 0)] * (center.ndim - 1) + [(4, 4)]
    ypad = jnp.pad(center, pad_spec)
    column = jnp.concatenate([top, center, bottom], axis=-3)
    total = 3.0 * weights[0] * center
    for offset in range(1, 5):
        total = total + weights[offset] * (
            wide[..., 4 + offset : 4 + offset + extent, :]
            + wide[..., 4 - offset : 4 - offset + extent, :]
        )
        total = total + weights[offset] * (
            ypad[..., 4 + offset : 4 + offset + across]
            + ypad[..., 4 - offset : 4 - offset + across]
        )
        total = total + weights[offset] * (
            column[..., 4 + offset : 4 + offset + depth, :, :]
            + column[..., 4 - offset : 4 - offset + depth, :, :]
        )
    return total


def source_field(src_cell, first_x, extent, depth, across):
    src_x = src_cell // across
    src_y = src_cell % across
    global_x = first_x + jnp.arange(extent, dtype=jnp.int32)
    ys = jnp.arange(across, dtype=jnp.int32)
    spot = (
        (global_x[None, :, None] == src_x[:, None, None])
        & (ys[None, None, :] == src_y[:, None, None])
    ).astype(jnp.float32)
    plane = (jnp.arange(depth, dtype=jnp.int32) == 0).astype(jnp.float32)
    return plane[None, :, None, None] * spot[:, None, :, :]


def shards(particles, loglik_grad, wave_prev, wave_now, ghosts, src_cell):
    own = particles.shape[0]
    depth = particles.shape[1]
    width = particles.shape[2]
    across = particles.shape[3]
    members = lax.axis_size("member")
    member_idx = lax.axis_index("member")
    space_idx = lax.axis_index("space")
    count = own * members
    every_x, every_g = (
        lax.all_gather(particles, "member", axis=0, tiled=True),
        lax.all_gather(loglik_grad, "member", axis=0, tiled=True),
    )
    xflat = every_x.reshape(count, -1)
    gflat = every_g.reshape(count, -1)
    first_row = member_idx * own
    gram = jnp.dot(
        xflat, xflat.T, precision=lax.Precision.HIGHEST, preferred_element_type=jnp.float32
    )
    norms = jnp.diagonal(gram)
    partial_dist = norms[:, None] + norms[None, :] - 2.0 * gram
    dist = lax.psum(partial_dist, "space")
    offdiag = 1.0 - jnp.eye(count, dtype=jnp.float32)
    band = jnp.sum(dist * offdiag) / (count * (count - 1) * math.log(count + 1))
    kern_rows = jnp.exp(-lax.dynamic_slice_in_dim(dist, first_row, own, 0) / band)
    kernel_grad = jnp.dot(
        kern_rows, gflat, precision=lax.Precision.HIGHEST, preferred_element_type=jnp.float32
    )
    kernel_pos = jnp.dot(
        kern_rows, xflat, precision=lax.Precision.HIGHEST, preferred_element_type=jnp.float32
    )
    mine = particles.reshape(own, -1)
    moved = mine + step_size * (
        0.5 * band * kernel_grad + jnp.sum(kern_rows, axis=1)[:, None] * mine - kernel_pos
    )
    new_particles = moved.reshape(particles.shape)
    coef = jnp.square(courant * (1.0 + 0.3 * jnp.tanh(particles)))
    inject = source_field(src_cell, space_idx * width, width, depth, across)
    top = ghosts[:, :GHOST]
    bottom = ghosts[:, GHOST:]
    prev = wave_prev
    now = wave_now
    for step in range(STEPS):
        wide = extended(now, (("space", 2),), GHOST)
        amplitude = 2.0 * math.cos(1.3 * step)
        following = 2.0 * now - prev + coef * laplace(wide, top, bottom) + amplitude * inject
        prev, now = (now, following)
    return (new_particles, prev, now)


def solution(mesh):
    placed = (
        P("member", None, "space", None),
        P("member", None, "space", None),
        P("member", None, "space", None),
        P("member", None, "space", None),
        P("member", None, "space", None),
        P("member"),
    )
    return jax.shard_map(
        shards,
        mesh=mesh,
        in_specs=placed,
        out_specs=(
            P("member", None, "space", None),
            P("member", None, "space", None),
            P("member", None, "space", None),
        ),
        check_vma=False,
    )
```

profile of v0, /device:TPU:0, one launch (start us, length us, event | category | flops | bytes accessed | tf_op | source)
XLA Modules:
  0.0 297.2 jit_solution(2316133455579283647)
XLA Ops:
  8.0 1.1 fusion.123
  9.1 2.4 collective-permute-start.1
  11.5 1.3 collective-permute-start
  13.0 7.1 %fusion.119 = (f32[8,4,25,800]{3,1,2,0:T(4,128)S(1)}, f32[8,4,25,800]{3,1,2,0:T(4,128)}) fusion(f32[8,8,25,800]{3,1,2,0:T(8,128)} %param.10), kind=kLoop, calls=%fused_computation.200 | loop fusion | bytes 10240000 | tf_op jit(solution)/shard_map/slice | solution.py:110
  22.4 19.3 %fusion.57 = (f32[8,2,25,800]{3,1,2,0:T(2,128)S(1)}, f32[8,2,25,800]{3,1,2,0:T(2,128)}, f32[8,2,25,800]{3,1,2,0:T(2,128)}, f32[8,2,25,800]{3,1,2,0:T(2,128)}, f3...) fusion(f32[8,2,25,800]{3,1,2,0:T(2,128)S(1)} %copy-done.13, f32[8,2,25,800]{3,1,2,0:T(2,128)S(1)} %copy-done.7, ...), kind=kLoop, calls=%fused_computation.82 | loop fusion | flops 16000000 | bytes 35200008 | tf_op jit(solution)/shard_map/add | solution.py:117
  41.7 1.1 copy-done.8
  42.9 5.5 %collective-permute-start.3 = (f32[8,2,4,800]{3,1,2,0:T(2,128)S(1)}, f32[8,2,4,800]{3,1,2,0:T(2,128)S(1)}, u32[]{:S(2)}, u32[]{:S(2)}) collective-permute-start(f32[8,2,4,800]{3,1,2,0:T(2,128)S(1)} %get-tuple-element.25), channel_id=1, source_target_pairs={{0,1},{1,2},{2,3},{3,4},{4,5},{5,6},{6,7},{8,9},{9,10},{10,11},{11... | collective-permute-start | bytes 614408 | tf_op jit(solution)/shard_map/ppermute | solution.py:25
  48.4 1.3 collective-permute-start.2
  49.7 1.2 copy.18
  50.9 2.1 collective-permute-done.2
  53.1 31.9 %fusion.58 = f32[8,2,25,800]{3,1,2,0:T(2,128)S(1)} fusion(f32[8,2,25,800]{3,1,2,0:T(2,128)} %param.9, f32[8,2,25,800]{3,1,2,0:T(2,128)} %copy-done.8, f32[8,2,25,800]{3,1,2,0:T(2,128)} %get-tuple-element.17, f32[8,2,4,800]{3,1,2,0:T(2,128)S(1)} %collective-permute-done.3, f32[8,2,4,800]{3,1,2,0:T(2,128)S(1)} %collective-permute-done.2, ...), kind=kLoop, calls=%fused_computation.83 | loop fusion | flops 16640000 | bytes 12569608 | tf_op jit(solution)/shard_map/add | solution.py:117
  85.1 7.7 %collective-permute-start.5 = (f32[8,2,4,800]{3,1,2,0:T(2,128)S(1)}, f32[8,2,4,800]{3,1,2,0:T(2,128)S(1)}, u32[]{:S(2)}, u32[]{:S(2)}) collective-permute-start(f32[8,2,4,800]{3,1,2,0:T(2,128)S(1)} %get-tuple-element.23), channel_id=1, source_target_pairs={{0,1},{1,2},{2,3},{3,4},{4,5},{5,6},{6,7},{8,9},{9,10},{10,11},{11... | collective-permute-start | bytes 614408 | tf_op jit(solution)/shard_map/ppermute | solution.py:25
  92.8 1.3 collective-permute-start.4
  94.1 2.1 collective-permute-done.4
  96.2 14.8 %fusion.59 = f32[8,2,25,800]{3,1,2,0:T(2,128)S(1)} fusion(f32[8,2,25,800]{3,1,2,0:T(2,128)S(1)} %copy-done.9, f32[8,2,25,800]{3,1,2,0:T(2,128)S(1)} %fusion.58, f32[8,2,25,800]{3,1,2,0:T(2,128)S(1)} %copy-done.5, f32[8,2,4,800]{3,1,2,0:T(2,128)S(1)} %collective-permute-done.5, f32[8,2,4,800]{3,1,2,0:T(2,128)S(1)} %collective-permute-done.4, ...), kind=kLoop, calls=%fused_computation.84 | loop fusion | flops 16640000 | bytes 12569608 | tf_op jit(solution)/shard_map/add | solution.py:117
  111.1 1.0 copy-done.12
  112.2 7.3 %collective-permute-start.7 = (f32[8,2,4,800]{3,1,2,0:T(2,128)S(1)}, f32[8,2,4,800]{3,1,2,0:T(2,128)S(1)}, u32[]{:S(2)}, u32[]{:S(2)}) collective-permute-start(f32[8,2,4,800]{3,1,2,0:T(2,128)S(1)} %get-tuple-element.21), channel_id=1, source_target_pairs={{0,1},{1,2},{2,3},{3,4},{4,5},{5,6},{6,7},{8,9},{9,10},{10,11},{11... | collective-permute-start | bytes 614408 | tf_op jit(solution)/shard_map/ppermute | solution.py:25
  119.5 1.5 collective-permute-start.6
  121.0 1.4 copy.17
  122.4 3.3 %reshape.86 = f32[8,40000]{1,0:T(8,128)} reshape(f32[8,2,25,800]{3,2,1,0:T(8,128)} %copy.17) | data formatting | bytes 2560000 | tf_op jit(solution)/shard_map/reshape | solution.py:103
  125.7 32.7 %fusion.60 = f32[8,2,25,800]{3,1,2,0:T(2,128)} fusion(f32[8,2,25,800]{3,1,2,0:T(2,128)} %copy-done.10, f32[8,2,25,800]{3,1,2,0:T(2,128)} %copy-done.12, f32[8,2,25,800]{3,1,2,0:T(2,128)} %get-tuple-element.17, f32[8,2,4,800]{3,1,2,0:T(2,128)S(1)} %collective-permute-done.7, f32[8,2,4,800]{3,1,2,0:T(2,128)S(1)} %collective-permute-done.6, ...), kind=kLoop, calls=%fused_computation.85 | loop fusion | flops 16640000 | bytes 12569608 | tf_op jit(solution)/shard_map/add | solution.py:117
  158.5 6.6 %copy.19 = f32[32,2,25,800]{3,2,1,0:T(8,128)} copy(f32[32,2,25,800]{3,1,2,0:T(2,128)} %all-gather.5.cloned.1.call-done) | data formatting | bytes 10240000 | tf_op jit(solution)/shard_map/all_gather | solution.py:83
  165.1 7.1 %reshape.87 = f32[32,40000]{1,0:T(8,128)} reshape(f32[32,2,25,800]{3,2,1,0:T(8,128)} %copy.19) | data formatting | bytes 10240000 | tf_op jit(solution)/shard_map/reshape | solution.py:86
  172.2 52.8 %all-gather.3.cloned.1.call-done = f32[32,2,25,800]{3,0,2,1:T(8,128)} async-done(((f32[8,2,25,800]{3,0,2,1:T(8,128)}), f32[32,2,25,800]{3,0,2,1:T(8,128)}) %all-gather.3.cloned.1.call-update) | async-done | bytes 5120016 | tf_op jit(solution)/shard_map/all_gather | solution.py:82
  225.0 9.2 %convolution_bitcast_fusion = f32[32,32]{1,0:T(8,128)S(1)} fusion(f32[32,2,25,800]{3,0,2,1:T(8,128)} %all-gather.3.cloned.1.call-done), kind=kOutput, calls=%fused_computation.182 | convolution fusion | flops 491520000 | bytes 5124096 | tf_op jit(solution)/shard_map/dot_general | solution.py:88
  235.0 24.1 %psum.7 = f32[32,32]{1,0:T(8,128)S(1)} all-reduce(f32[32,32]{1,0:T(8,128)S(1)} %multiply_subtract_fusion), channel_id=1, replica_groups=mesh['member'=4,'space'=8] {'space'}, use_global_device_ids=true, to_apply=%region_0.1 | all-reduce | flops 1024 | bytes 8192 | tf_op jit(solution)/shard_map/psum | solution.py:93
  261.0 8.9 %copy.20 = f32[32,2,25,800]{3,2,1,0:T(8,128)} copy(f32[32,2,25,800]{3,0,2,1:T(8,128)} %all-gather.3.cloned.1.call-done) | data formatting | bytes 10240000 | tf_op jit(solution)/shard_map/all_gather | solution.py:82
  269.9 7.2 %reshape.88 = f32[32,40000]{1,0:T(8,128)} reshape(f32[32,2,25,800]{3,2,1,0:T(8,128)} %copy.20) | data formatting | bytes 10240000 | tf_op jit(solution)/shard_map/reshape | solution.py:85
  277.2 4.6 %fusion = f32[8,40000]{1,0:T(8,128)S(1)} fusion(f32[32,40000]{1,0:T(8,128)} %reshape.87, f32[8,40000]{1,0:T(8,128)S(1)} %copy-done.11, f32[8]{0:T(128)S(1)} %fusion.118, f32[]{:T(128)S(6)} %mul_shard_map.3, f32[32,32]{1,0:T(8,128)S(1)} %psum.7, s32[]{:T(128)S(6)} %select_n.19, f32[]{:T(128)S(6)} %div.15), kind=kOutput, calls=%fused_computation.3 | convolution fusion | flops 123840512 | bytes 7686668 | tf_op jit(solution)/shard_map/dot_general | solution.py:97
  281.8 3.7 %fusion.2 = f32[8,40000]{1,0:T(8,128)} fusion(f32[8,40000]{1,0:T(8,128)S(1)} %copy-done.11, f32[8,40000]{1,0:T(8,128)S(1)} %fusion, f32[32,40000]{1,0:T(8,128)S(1)} %copy-done.6, f32[32,32]{1,0:T(8,128)S(1)} %psum.7, s32[]{:T(128)S(6)} %select_n.19, f32[]{:T(128)S(6)} %div.15), kind=kOutput, calls=%fused_computation.5 | convolution fusion | flops 123840512 | bytes 8976392 | tf_op jit(solution)/shard_map/dot_general | solution.py:100
  285.5 2.6 reshape.89
  288.1 2.2 copy.21
  (61 shorter events, 4.9 us)
Async XLA Ops:
  7.2 5.7 %copy-start.14 = (s32[8]{0:T(128)S(1)}, s32[8]{0:T(128)}, u32[]{:S(2)}) copy-start(s32[8]{0:T(128)} %param.11) | copy-start | bytes 100
  7.2 151.3 %all-gather.5.cloned.1.call-start = ((), (), s32[]{:S(2)}) async-start(), calls=%async_computation.1 | async-start | bytes 7168000 | tf_op jit(solution)/shard_map/all_gather | solution.py:83
  7.9 217.1 %all-gather.3.cloned.1.call-start = ((), (), s32[]{:S(2)}) async-start(), calls=%async_computation | async-start | bytes 7168000 | tf_op jit(solution)/shard_map/all_gather | solution.py:82
  9.1 11.2 %collective-permute-start.1 = (f32[8,2,4,800]{3,1,2,0:T(2,128)S(1)}, f32[8,2,4,800]{3,1,2,0:T(2,128)S(1)}, u32[]{:S(2)}, u32[]{:S(2)}) collective-permute-start(f32[8,2,4,800]{3,1,2,0:T(2,128)S(1)} %get-tuple-element.27), channel_id=1, source_target_pairs={{0,1},{1,2},{2,3},{3,4},{4,5},{5,6},{6,7},{8,9},{9,10},{10,11},{11... | collective-permute-start | bytes 614408 | tf_op jit(solution)/shard_map/ppermute | solution.py:25
  11.5 9.7 %collective-permute-start = (f32[8,2,4,800]{3,1,2,0:T(2,128)S(1)}, f32[8,2,4,800]{3,1,2,0:T(2,128)S(1)}, u32[]{:S(2)}, u32[]{:S(2)}) collective-permute-start(f32[8,2,4,800]{3,1,2,0:T(2,128)S(1)} %get-tuple-element.26), channel_id=1, source_target_pairs={{1,0},{2,1},{3,2},{4,3},{5,4},{6,5},{7,6},{9,8},{10,9},{11,10},{12... | collective-permute-start | bytes 614408 | tf_op jit(solution)/shard_map/ppermute | solution.py:27
  12.9 8.4 %slice-start = ((s8[5734400]{0:T(1024)(128)(4,1)}), s8[4194304]{0:T(1024)(128)(4,1)S(1)}, s32[]{:S(2)}) async-start(s8[5734400]{0:T(1024)(128)(4,1)} %bitcast.10), calls=%async_computation.2 | async-start | bytes 8388608
  13.0 7.3 %copy-start.7 = (f32[8,2,25,800]{3,1,2,0:T(2,128)S(1)}, f32[8,2,25,800]{3,1,2,0:T(2,128)}, u32[]{:S(2)}) copy-start(f32[8,2,25,800]{3,1,2,0:T(2,128)} %param.9) | copy-start | bytes 3840004
  13.0 8.3 %slice-start.1 = ((s8[5734400]{0:T(1024)(128)(4,1)}), s8[1540096]{0:T(1024)(128)(4,1)S(1)}, s32[]{:S(2)}) async-start(s8[5734400]{0:T(1024)(128)(4,1)} %bitcast.10), calls=%async_computation.3 | async-start | bytes 3080192
  20.3 1.5 copy-start
  20.3 2.0 copy-start.13
  41.7 1.1 copy-start.8
  42.9 8.1 %collective-permute-start.3 = (f32[8,2,4,800]{3,1,2,0:T(2,128)S(1)}, f32[8,2,4,800]{3,1,2,0:T(2,128)S(1)}, u32[]{:S(2)}, u32[]{:S(2)}) collective-permute-start(f32[8,2,4,800]{3,1,2,0:T(2,128)S(1)} %get-tuple-element.25), channel_id=1, source_target_pairs={{0,1},{1,2},{2,3},{3,4},{4,5},{5,6},{6,7},{8,9},{9,10},{10,11},{11... | collective-permute-start | bytes 614408 | tf_op jit(solution)/shard_map/ppermute | solution.py:25
  48.4 4.6 %collective-permute-start.2 = (f32[8,2,4,800]{3,1,2,0:T(2,128)S(1)}, f32[8,2,4,800]{3,1,2,0:T(2,128)S(1)}, u32[]{:S(2)}, u32[]{:S(2)}) collective-permute-start(f32[8,2,4,800]{3,1,2,0:T(2,128)S(1)} %get-tuple-element.24), channel_id=1, source_target_pairs={{1,0},{2,1},{3,2},{4,3},{5,4},{6,5},{7,6},{9,8},{10,9},{11,10},{12... | collective-permute-start | bytes 614408 | tf_op jit(solution)/shard_map/ppermute | solution.py:27
  53.1 43.1 %copy-start.1 = (f32[8,2,25,800]{3,1,2,0:T(2,128)S(1)}, f32[8,2,25,800]{3,1,2,0:T(2,128)}, u32[]{:S(2)}) copy-start(f32[8,2,25,800]{3,1,2,0:T(2,128)} %get-tuple-element.13) | copy-start | bytes 3840004
  53.1 43.1 %copy-start.2 = (f32[8,2,25,800]{3,1,2,0:T(2,128)S(1)}, f32[8,2,25,800]{3,1,2,0:T(2,128)}, u32[]{:S(2)}) copy-start(f32[8,2,25,800]{3,1,2,0:T(2,128)} %get-tuple-element.14) | copy-start | bytes 3840004
  53.1 43.1 %copy-start.3 = (f32[8,2,25,800]{3,1,2,0:T(2,128)S(1)}, f32[8,2,25,800]{3,1,2,0:T(2,128)}, u32[]{:S(2)}) copy-start(f32[8,2,25,800]{3,1,2,0:T(2,128)} %get-tuple-element.15) | copy-start | bytes 3840004
  53.1 43.1 %copy-start.4 = (f32[8,2,25,800]{3,1,2,0:T(2,128)S(1)}, f32[8,2,25,800]{3,1,2,0:T(2,128)}, u32[]{:S(2)}) copy-start(f32[8,2,25,800]{3,1,2,0:T(2,128)} %get-tuple-element.16) | copy-start | bytes 3840004
  53.1 43.1 %copy-start.5 = (f32[8,2,25,800]{3,1,2,0:T(2,128)S(1)}, f32[8,2,25,800]{3,1,2,0:T(2,128)}, u32[]{:S(2)}) copy-start(f32[8,2,25,800]{3,1,2,0:T(2,128)} %get-tuple-element.17) | copy-start | bytes 3840004
  53.1 43.1 %copy-start.9 = (f32[8,2,25,800]{3,1,2,0:T(2,128)S(1)}, f32[8,2,25,800]{3,1,2,0:T(2,128)}, u32[]{:S(2)}) copy-start(f32[8,2,25,800]{3,1,2,0:T(2,128)} %copy-done.8) | copy-start | bytes 3840004
  85.0 26.0 %copy-start.10 = (f32[8,2,25,800]{3,1,2,0:T(2,128)}, f32[8,2,25,800]{3,1,2,0:T(2,128)S(1)}, u32[]{:S(2)}) copy-start(f32[8,2,25,800]{3,1,2,0:T(2,128)S(1)} %fusion.58) | copy-start | bytes 3840004
  85.1 9.0 %collective-permute-start.5 = (f32[8,2,4,800]{3,1,2,0:T(2,128)S(1)}, f32[8,2,4,800]{3,1,2,0:T(2,128)S(1)}, u32[]{:S(2)}, u32[]{:S(2)}) collective-permute-start(f32[8,2,4,800]{3,1,2,0:T(2,128)S(1)} %get-tuple-element.23), channel_id=1, source_target_pairs={{0,1},{1,2},{2,3},{3,4},{4,5},{5,6},{6,7},{8,9},{9,10},{10,11},{11... | collective-permute-start | bytes 614408 | tf_op jit(solution)/shard_map/ppermute | solution.py:25
  92.8 3.4 %collective-permute-start.4 = (f32[8,2,4,800]{3,1,2,0:T(2,128)S(1)}, f32[8,2,4,800]{3,1,2,0:T(2,128)S(1)}, u32[]{:S(2)}, u32[]{:S(2)}) collective-permute-start(f32[8,2,4,800]{3,1,2,0:T(2,128)S(1)} %get-tuple-element.22), channel_id=1, source_target_pairs={{1,0},{2,1},{3,2},{4,3},{5,4},{6,5},{7,6},{9,8},{10,9},{11,10},{12... | collective-permute-start | bytes 614408 | tf_op jit(solution)/shard_map/ppermute | solution.py:27
  111.1 1.1 copy-start.12
  112.2 13.5 %collective-permute-start.7 = (f32[8,2,4,800]{3,1,2,0:T(2,128)S(1)}, f32[8,2,4,800]{3,1,2,0:T(2,128)S(1)}, u32[]{:S(2)}, u32[]{:S(2)}) collective-permute-start(f32[8,2,4,800]{3,1,2,0:T(2,128)S(1)} %get-tuple-element.21), channel_id=1, source_target_pairs={{0,1},{1,2},{2,3},{3,4},{4,5},{5,6},{6,7},{8,9},{9,10},{10,11},{11... | collective-permute-start | bytes 614408 | tf_op jit(solution)/shard_map/ppermute | solution.py:25
  119.5 6.2 %collective-permute-start.6 = (f32[8,2,4,800]{3,1,2,0:T(2,128)S(1)}, f32[8,2,4,800]{3,1,2,0:T(2,128)S(1)}, u32[]{:S(2)}, u32[]{:S(2)}) collective-permute-start(f32[8,2,4,800]{3,1,2,0:T(2,128)S(1)} %get-tuple-element.20), channel_id=1, source_target_pairs={{1,0},{2,1},{3,2},{4,3},{5,4},{6,5},{7,6},{9,8},{10,9},{11,10},{12... | collective-permute-start | bytes 614408 | tf_op jit(solution)/shard_map/ppermute | solution.py:27
  269.9 7.3 %copy-start.11 = (f32[8,40000]{1,0:T(8,128)S(1)}, f32[8,40000]{1,0:T(8,128)}, u32[]{:S(2)}) copy-start(f32[8,40000]{1,0:T(8,128)} %reshape.86) | copy-start | bytes 3840004
  277.2 4.6 %copy-start.6 = (f32[32,40000]{1,0:T(8,128)S(1)}, f32[32,40000]{1,0:T(8,128)}, u32[]{:S(2)}) copy-start(f32[32,40000]{1,0:T(8,128)} %reshape.88) | copy-start | bytes 15360004
Sparse Core Ops, SparseCore 0:
  9.6 108.8 all-gather.4
  120.6 104.3 all-gather.2
where the time goes:
time: 298 us; the launch traced here: 297 us
  other arithmetic  99.9 us (34%)
  waiting for transfers between devices  57.8 us (19%)
  local copies, waits for them, and re-layouts  53.8 us (18%)
  starting transfers between devices  28.4 us (10%)
  blocking collectives  24.1 us (8%)
  matrix products  17.4 us (6%)
  between operations  15.7 us (5%)
    add x4, other arithmetic, shards(): 2.0 * now - prev + coef * laplace(wide, top, bottom) + amplitude * inject  98.8 us
    all_gather x1, waiting for transfers between devices, shards(): lax.all_gather(particles, 'member', axis=0, tiled=True)  52.8 us
    psum x1, blocking collectives, shards(): dist = lax.psum(partial_dist, 'space')  24.1 us
    ppermute x4, starting transfers between devices, extended(): lax.ppermute(tail, axis, [(i, (i + 1) % count) for i in range(ends)])  22.9 us
    dot_general x1, matrix products, shards(): jnp.dot(xflat, xflat.T, precision=lax.Precision.HIGHEST, preferred_elemen...  9.16 us
    unnamed x39, local copies, waits for them, and re-layouts  8.95 us
    all_gather x1, local copies, waits for them, and re-layouts, shards(): lax.all_gather(particles, 'member', axis=0, tiled=True)  8.94 us
    reshape x1, local copies, waits for them, and re-layouts, shards(): xflat = every_x.reshape(count, -1)  7.16 us
  transfers between devices with their start and end apart: 10, of which 3 were waited for; matrix products, arithmetic and copies ran while one was open for 43% of the time, Pallas kernels for 0%

commit v1 on v0

v1 whole, which is shorter than its diff:
```python
import functools
import math

import jax
import jax.numpy as jnp
from jax import lax
from jax.experimental import pallas as pl
from jax.experimental.pallas import tpu as pltpu
from jax.sharding import PartitionSpec as P

GHOST = 4
STEPS = 4
LANES = 128

weights = (-205.0 / 72.0, 8.0 / 5.0, -1.0 / 5.0, 8.0 / 315.0, -1.0 / 560.0)
step_size = 0.25
courant = 0.3

VMEM = pl.BlockSpec(memory_space=pltpu.VMEM)
SMEM = pl.BlockSpec(memory_space=pltpu.SMEM)


def params():
    return pltpu.CompilerParams(vmem_limit_bytes=40 << 20)


class Packing:
    def __init__(self, width, depth, across, members):
        self.width, self.depth, self.across, self.members = width, depth, across, members
        self.rows = width * depth
        self.full = across // LANES
        self.tail = across % LANES
        self.group = LANES // self.tail if self.tail else 1
        self.tail_tiles = -(-self.rows // self.group) if self.tail else 0
        total = self.rows * self.full + self.tail_tiles
        self.tiles = -(-total // members)
        self.lanes = self.tiles * LANES
        self.spare = self.tiles * members - total

    def runs(self, row):
        tile, at, left = row * self.full, 0, self.full
        while left:
            chunk, place = divmod(tile, self.tiles)
            count = min(left, self.tiles - place)
            yield chunk, place * LANES, at * LANES, count * LANES
            tile, at, left = tile + count, at + count, left - count

    def tail_place(self, index):
        chunk, place = divmod(self.rows * self.full + index, self.tiles)
        return chunk, place * LANES


def pack_body(pack, cuts, me_ref, cells_ref, *refs):
    outs, buf = refs[:-1], refs[-1]
    own = cells_ref.shape[2]
    me = me_ref[0]
    slots = [lax.rem(chunk - me + pack.members, pack.members) for chunk in range(pack.members)]
    for row in range(pack.rows):
        x, z = divmod(row, pack.depth)
        for chunk, there, here, count in pack.runs(row):
            buf[slots[chunk], :, there : there + count] = cells_ref[x, z, :, here : here + count]
    start = pack.full * LANES
    for index in range(pack.tail_tiles):
        chunk, place = pack.tail_place(index)
        pieces = []
        for row in range(index * pack.group, min(pack.rows, (index + 1) * pack.group)):
            x, z = divmod(row, pack.depth)
            pieces.append(cells_ref[x, z, :, start : start + pack.tail])
        empty = LANES - pack.tail * len(pieces)
        if empty:
            pieces.append(jnp.zeros((own, empty), jnp.float32))
        buf[slots[chunk], :, place : place + LANES] = jnp.concatenate(pieces, axis=1)
    for index in range(pack.spare):
        chunk, place = pack.tail_place(pack.tail_tiles + index)
        buf[slots[chunk], :, place : place + LANES] = jnp.zeros((own, LANES), jnp.float32)
    at = 0
    for low, high in cuts:
        for slot in range(pack.members):
            outs[at][...] = buf[slot, :, low:high]
            at += 1


def packed(pack, cuts, me, cells):
    own = cells.shape[2]
    outs = pl.pallas_call(
        functools.partial(pack_body, pack, cuts),
        out_shape=[
            jax.ShapeDtypeStruct((own, high - low), jnp.float32)
            for low, high in cuts
            for _ in range(pack.members)
        ],
        in_specs=[SMEM, VMEM],
        out_specs=[VMEM] * (len(cuts) * pack.members),
        scratch_shapes=[pltpu.VMEM((pack.members, own, pack.lanes), jnp.float32)],
        compiler_params=params(),
        name="pack",
    )(me, cells)
    return [outs[i * pack.members : (i + 1) * pack.members] for i in range(len(cuts))]


def unpack_body(pack, cuts, me_ref, *refs):
    parts, out_ref, buf = refs[:-2], refs[-2], refs[-1]
    me = me_ref[0]
    at = 0
    for low, high in cuts:
        for shift in range(pack.members):
            chunk = lax.rem(me - shift + pack.members, pack.members)
            buf[chunk, :, low:high] = parts[at][...]
            at += 1
    for row in range(pack.rows):
        x, z = divmod(row, pack.depth)
        for chunk, there, here, count in pack.runs(row):
            out_ref[x, z, :, here : here + count] = buf[chunk, :, there : there + count]
    start = pack.full * LANES
    for index in range(pack.tail_tiles):
        chunk, place = pack.tail_place(index)
        tile = buf[chunk, :, place : place + LANES]
        for k, row in enumerate(range(index * pack.group, min(pack.rows, (index + 1) * pack.group))):
            x, z = divmod(row, pack.depth)
            out_ref[x, z, :, start : start + pack.tail] = tile[:, k * pack.tail : (k + 1) * pack.tail]


def unpacked(pack, cuts, me, parts):
    own = parts[0].shape[0]
    return pl.pallas_call(
        functools.partial(unpack_body, pack, cuts),
        out_shape=jax.ShapeDtypeStruct((pack.width, pack.depth, own, pack.across), jnp.float32),
        in_specs=[SMEM] + [VMEM] * len(parts),
        out_specs=VMEM,
        scratch_shapes=[pltpu.VMEM((pack.members, own, pack.lanes), jnp.float32)],
        compiler_params=params(),
        name="unpack",
    )(me, *parts)


def distance_body(members, me_ref, *refs):
    parts, out_ref, all_ref = refs[:members], refs[members], refs[members + 1]
    own = parts[0].shape[0]
    me = me_ref[0]
    for shift in range(members):
        row = pl.multiple_of(lax.rem(me - shift + members, members) * own, own)
        all_ref[pl.ds(row, own), :] = parts[shift][...]
    cells = all_ref[...]
    cells = cells - cells[0:1, :]
    gram = lax.dot_general(
        cells,
        cells,
        (((1,), (1,)), ((), ())),
        precision=lax.Precision.HIGHEST,
        preferred_element_type=jnp.float32,
    )
    count = gram.shape[0]
    rows = lax.broadcasted_iota(jnp.int32, (count, count), 0)
    cols = lax.broadcasted_iota(jnp.int32, (count, count), 1)
    diag = jnp.where(rows == cols, gram, 0.0)
    down = jnp.sum(diag, axis=1, keepdims=True)
    along = jnp.sum(diag, axis=0, keepdims=True)
    out_ref[...] = jnp.where(rows == cols, 0.0, down + along - 2.0 * gram)


def distances(members, me, parts):
    own, lanes = parts[0].shape
    count = own * members
    return pl.pallas_call(
        functools.partial(distance_body, members),
        out_shape=jax.ShapeDtypeStruct((count, count), jnp.float32),
        in_specs=[SMEM] + [VMEM] * members,
        out_specs=VMEM,
        scratch_shapes=[pltpu.VMEM((count, lanes), jnp.float32)],
        compiler_params=params(),
        name="distances",
    )(me, *parts)


def update_body(members, low, me_ref, dist_ref, *refs):
    cells, grads = refs[:members], refs[members : 2 * members]
    outs = refs[2 * members : 3 * members]
    cell_ref, grad_ref, out_ref = refs[3 * members :]
    own, lanes = grads[0].shape
    count = own * members
    me = me_ref[0]
    for shift in range(members):
        row = pl.multiple_of(lax.rem(me - shift + members, members) * own, own)
        cell_ref[pl.ds(row, own), :] = cells[shift][:, low : low + lanes]
        grad_ref[pl.ds(row, own), :] = grads[shift][...]
    dist = dist_ref[...]
    band = jnp.sum(jnp.sum(dist, axis=1, keepdims=True), axis=0, keepdims=True) / (
        count * (count - 1) * math.log(count + 1)
    )
    kern = jnp.exp(-dist / band)
    total = jnp.sum(kern, axis=1, keepdims=True)
    cell = cell_ref[...]
    mixed = 0.5 * band * grad_ref[...] - cell
    pulled = jnp.dot(
        kern, mixed, precision=lax.Precision.HIGHEST, preferred_element_type=jnp.float32
    )
    out_ref[...] = cell + step_size * (pulled + total * cell)
    for shift in range(members):
        row = pl.multiple_of(lax.rem(me + shift, members) * own, own)
        outs[shift][...] = out_ref[pl.ds(row, own), :]


def updated(members, low, me, dist, cells, grads):
    own, lanes = grads[0].shape
    count = own * members
    return pl.pallas_call(
        functools.partial(update_body, members, low),
        out_shape=[jax.ShapeDtypeStruct((own, lanes), jnp.float32)] * members,
        in_specs=[SMEM, VMEM] + [VMEM] * (2 * members),
        out_specs=[VMEM] * members,
        scratch_shapes=[pltpu.VMEM((count, lanes), jnp.float32)] * 3,
        compiler_params=params(),
        name="update",
    )(me, dist, *cells, *grads)


def exchange(parts, members):
    return [parts[0]] + [
        lax.ppermute(parts[shift], "member", [(i, (i + shift) % members) for i in range(members)])
        for shift in range(1, members)
    ]


def medium_body(across, cells_ref, ghosts_ref, coef_ref, still_ref):
    width, depth, own, _ = cells_ref.shape
    lanes = coef_ref.shape[-1]
    start = (across // LANES) * LANES
    if lanes > start:
        edge = jnp.zeros((own, lanes - start), jnp.float32)

    def one(x, carry):
        for z in range(depth):
            if lanes > start:
                coef_ref[x, z, :, start:] = edge
                still_ref[x, z, :, start:] = edge
            speed = courant * (1.0 + 0.3 * jnp.tanh(cells_ref[x, z]))
            coef_ref[x, z, :, :across] = speed * speed
            total = None
            for offset in range(1, GHOST + 1):
                terms = []
                if z - offset < 0:
                    terms.append(ghosts_ref[x, GHOST + z - offset])
                if z + offset >= depth:
                    terms.append(ghosts_ref[x, GHOST + z + offset - depth])
                for term in terms:
                    part = weights[offset] * term
                    total = part if total is None else total + part
            if total is None:
                total = jnp.zeros((own, across), jnp.float32)
            still_ref[x, z, :, :across] = total
        return carry

    lax.fori_loop(0, width, one, 0)


def medium(across, lanes, cells, ghosts):
    shape = jax.ShapeDtypeStruct(cells.shape[:3] + (lanes,), jnp.float32)
    return pl.pallas_call(
        functools.partial(medium_body, across),
        out_shape=[shape, shape],
        in_specs=[VMEM, VMEM],
        out_specs=[VMEM, VMEM],
        compiler_params=params(),
        name="medium",
    )(cells, ghosts)


def wave_body(amplitude, last, source_ref, left_ref, right_ref, now_ref, prev_ref, coef_ref, still_ref, *refs):
    out_ref, wide = refs[0], refs[-1]
    width, depth, own, lanes = now_ref.shape
    wide[0:GHOST] = left_ref[...]
    wide[GHOST : GHOST + width] = now_ref[...]
    wide[GHOST + width :] = right_ref[...]

    def one(x, carry):
        for z in range(depth):
            center = wide[x + GHOST, z]
            total = 3.0 * weights[0] * center + still_ref[x, z]
            for offset in range(1, GHOST + 1):
                pair = wide[x + GHOST + offset, z] + wide[x + GHOST - offset, z]
                pair = pair + pltpu.roll(center, offset, 1) + pltpu.roll(center, lanes - offset, 1)
                if z - offset >= 0:
                    pair = pair + wide[x + GHOST, z - offset]
                if z + offset < depth:
                    pair = pair + wide[x + GHOST, z + offset]
                total = total + weights[offset] * pair
            out_ref[x, z] = 2.0 * center - prev_ref[x, z] + coef_ref[x, z] * total
        return carry

    lax.fori_loop(0, width, one, 0)
    rows = lax.broadcasted_iota(jnp.int32, (own, lanes), 0)
    cols = lax.broadcasted_iota(jnp.int32, (own, lanes), 1)
    for index in range(own):
        x, y = source_ref[0, index], source_ref[1, index]

        @pl.when((x >= 0) & (x < width))
        def _(x=x, y=y, index=index):
            spot = (rows == index) & (cols == y)
            out_ref[x, 0] = out_ref[x, 0] + jnp.where(spot, amplitude, 0.0)

    if not last:
        head_ref, tail_ref = refs[1], refs[2]
        head_ref[...] = out_ref[0:GHOST]
        tail_ref[...] = out_ref[width - GHOST :]


def wave_step(amplitude, last, source, left, right, now, prev, coef, still):
    width, depth, own, lanes = now.shape
    out = jax.ShapeDtypeStruct(now.shape, jnp.float32)
    edge = jax.ShapeDtypeStruct((GHOST,) + now.shape[1:], jnp.float32)
    outs = [out] if last else [out, edge, edge]
    return pl.pallas_call(
        functools.partial(wave_body, amplitude, last),
        out_shape=outs,
        in_specs=[SMEM] + [VMEM] * 6,
        out_specs=[VMEM] * len(outs),
        scratch_shapes=[pltpu.VMEM((width + 2 * GHOST, depth, own, lanes), jnp.float32)],
        compiler_params=params(),
        name="wave",
    )(source, left, right, now, prev, coef, still)


def shards(cuts_of, particles, loglik_grad, wave_prev, wave_now, ghosts, src_cell):
    own, depth, width, across = particles.shape
    members = lax.axis_size("member")
    spaces = lax.axis_size("space")
    member_idx = lax.axis_index("member")
    space_idx = lax.axis_index("space")
    pack = Packing(width, depth, across, members)
    whole = [(0, pack.lanes)]
    cuts = cuts_of(pack)
    me = jnp.reshape(member_idx, (1,)).astype(jnp.int32)
    lanes = -(-(across + GHOST) // LANES) * LANES

    def turned(array):
        return jnp.transpose(array, (2, 1, 0, 3))

    cells = turned(particles)
    cell_parts = exchange(packed(pack, whole, me, cells)[0], members)
    grad_parts = [exchange(part, members) for part in packed(pack, cuts, me, turned(loglik_grad))]

    dist = distances(members, me, cell_parts)
    dist = jnp.sum(lax.all_gather(dist, "space", axis=0), axis=0)
    dist = sum(exchange([dist] * members, members))

    moved = []
    for (low, _), grads in zip(cuts, grad_parts):
        moved += exchange(updated(members, low, me, dist, cell_parts, grads), members)
    new_particles = turned(unpacked(pack, cuts, me, moved))

    def wide(array):
        return jnp.pad(turned(array), ((0, 0), (0, 0), (0, 0), (0, lanes - across)))

    source = jnp.stack([src_cell // across - space_idx * width, src_cell % across])
    coef, still = medium(across, lanes, cells, turned(ghosts))
    prev, now = wide(wave_prev), wide(wave_now)
    head, tail = now[:GHOST], now[width - GHOST :]
    for step in range(STEPS):
        left = lax.ppermute(tail, "space", [(i, i + 1) for i in range(spaces - 1)])
        right = lax.ppermute(head, "space", [(i + 1, i) for i in range(spaces - 1)])
        amplitude = 2.0 * math.cos(1.3 * step)
        last = step == STEPS - 1
        outs = wave_step(amplitude, last, source, left, right, now, prev, coef, still)
        if not last:
            head, tail = outs[1], outs[2]
        prev, now = now, outs[0]
    return new_particles, turned(prev[..., :across]), turned(now[..., :across])


def one_cut(pack):
    return [(0, pack.lanes)]


def solution(mesh):
    spec = P("member", None, "space", None)
    return jax.shard_map(
        functools.partial(shards, one_cut),
        mesh=mesh,
        in_specs=(spec, spec, spec, spec, spec, P("member")),
        out_specs=(spec, spec, spec),
        check_vma=False,
    )
```

time: 298 us -> 138 us (0.46)
  the two profiles are of different devices: /device:TPU:0 before, /device:TPU:9 now
where the time goes in v1:
time: 138 us
  waiting for transfers between devices  39.4 us (29%)
  starting transfers between devices  38.6 us (28%)
  Pallas kernels  29.4 us (21%)
  local copies, waits for them, and re-layouts  19.7 us (14%)
  blocking collectives  9.63 us (7%)
    ppermute x12, waiting for transfers between devices, exchange(): lax.ppermute(parts[shift], 'member', [(i, (i + shift) % members) for i in...  35.9 us
    pallas_call x4, Pallas kernels, wave_step(): pl.pallas_call(functools.partial(wave_body, amplitude, last), out_shape=o...  23.1 us
    ppermute x4, starting transfers between devices, shards(): left = lax.ppermute(tail, 'space', [(i, i + 1) for i in range(spaces - 1)])  18.4 us
    unnamed x20, local copies, waits for them, and re-layouts  17.1 us
    ppermute x12, starting transfers between devices, exchange(): lax.ppermute(parts[shift], 'member', [(i, (i + shift) % members) for i in...  12.5 us
    all_gather x1, blocking collectives, shards(): dist = jnp.sum(lax.all_gather(dist, 'space', axis=0), axis=0)  9.63 us
    ppermute x4, starting transfers between devices, shards(): right = lax.ppermute(head, 'space', [(i + 1, i) for i in range(spaces - 1)])  7.68 us
    ppermute x4, waiting for transfers between devices, shards(): right = lax.ppermute(head, 'space', [(i + 1, i) for i in range(spaces - 1)])  3.48 us
  transfers between devices with their start and end apart: 20, of which 6 were waited for; matrix products, arithmetic and copies ran while one was open for 9% of the time, Pallas kernels for 12%

profile of v1, /device:TPU:9, one launch (start us, length us, event | category | flops | bytes accessed | tf_op | source)
XLA Modules:
  0.0 137.6 jit_solution(3423159061130971193)
XLA Ops:
  0.6 1.5 %copy.26 = f32[8,2,25,800]{3,0,1,2:T(8,128)S(1)} copy(f32[8,2,25,800]{3,1,2,0:T(2,128)} %param.6) | data formatting | bytes 2560000 | tf_op args[0]
  3.1 1.3 collective-permute-start
  5.4 1.5 %collective-permute-start.2 = (f32[8,10112]{1,0:T(8,128)}, f32[8,10112]{1,0:T(8,128)S(1)}, u32[]{:S(2)}, u32[]{:S(2)}) collective-permute-start(f32[8,10112]{1,0:T(8,128)} %get-tuple-element.29), channel_id=1, source_target_pairs={{0,24},{8,0},{16,8},{24,16},{1,25},{9,1},{17,9},{25,17},{2,26},{10... | collective-permute-start | bytes 970760 | tf_op jit(solution)/shard_map/ppermute | solution.py:219
  6.9 1.5 %copy.24 = f32[8,2,25,800]{3,0,1,2:T(8,128)S(1)} copy(f32[8,2,25,800]{3,1,2,0:T(2,128)} %param.9) | data formatting | bytes 2560000 | tf_op args[3]
  10.3 4.5 %collective-permute-start.12 = (f32[4,2,8,896]{3,2,1,0:T(8,128)}, f32[4,2,8,896]{3,2,1,0:T(8,128)}, u32[]{:S(2)}, u32[]{:S(2)}) collective-permute-start(f32[4,2,8,896]{3,2,1,0:T(8,128)} %get-tuple-element.53), channel_id=1, source_target_pairs={{0,1},{1,2},{2,3},{3,4},{4,5},{5,6},{6,7},{8,9},{9,10},{10,11},{11... | collective-permute-start | bytes 688136 | tf_op jit(solution)/shard_map/ppermute | solution.py:359
  14.8 1.9 %collective-permute-start.13 = (f32[4,2,8,896]{3,2,1,0:T(8,128)}, f32[4,2,8,896]{3,2,1,0:T(8,128)}, u32[]{:S(2)}, u32[]{:S(2)}) collective-permute-start(f32[4,2,8,896]{3,2,1,0:T(8,128)} %get-tuple-element.52), channel_id=1, source_target_pairs={{1,0},{2,1},{3,2},{4,3},{5,4},{6,5},{7,6},{9,8},{10,9},{11,10},{12... | collective-permute-start | bytes 688136 | tf_op jit(solution)/shard_map/ppermute | solution.py:360
  16.7 1.5 %copy.25 = f32[8,2,25,800]{3,0,1,2:T(8,128)S(1)} copy(f32[8,2,25,800]{3,1,2,0:T(2,128)} %param.7) | data formatting | bytes 2560000 | tf_op args[1]
  20.6 12.4 %collective-permute-done.1.refs_2_ = f32[8,10112]{1,0:T(8,128)S(1)} collective-permute-done((f32[8,10112]{1,0:T(8,128)}, f32[8,10112]{1,0:T(8,128)S(1)}, u32[]{:S(2)}, u32[]{:S(2)}) %collective-permute-start.1) | collective-permute-done | bytes 323616 | tf_op jit(solution)/shard_map/ppermute | solution.py:219
  33.0 3.5 %collective-permute-start.7 = (f32[8,10112]{1,0:T(8,128)}, f32[8,10112]{1,0:T(8,128)}, u32[]{:S(2)}, u32[]{:S(2)}) collective-permute-start(f32[8,10112]{1,0:T(8,128)} %copy-done.1), channel_id=1, source_target_pairs={{0,16},{8,24},{16,0},{24,8},{1,17},{9,25},{17,1},{25,9},{2,18},{10... | collective-permute-start | bytes 970760 | tf_op jit(solution)/shard_map/ppermute | solution.py:219
  36.5 8.3 %collective-permute-done.2.refs_3_ = f32[8,10112]{1,0:T(8,128)S(1)} collective-permute-done((f32[8,10112]{1,0:T(8,128)}, f32[8,10112]{1,0:T(8,128)S(1)}, u32[]{:S(2)}, u32[]{:S(2)}) %collective-permute-start.2) | collective-permute-done | bytes 323616 | tf_op jit(solution)/shard_map/ppermute | solution.py:219
  46.0 9.6 %all-gather = f32[256,32]{1,0:T(8,128)S(1)} all-gather(f32[32,32]{1,0:T(8,128)S(1)} %distances.1), channel_id=2, replica_groups=mesh['member'=4,'space'=8] {'space'}, dimensions={0}, use_global_device_ids=true | all-gather | bytes 36864 | tf_op jit(solution)/shard_map/all_gather | solution.py:343
  55.8 1.5 %collective-permute-start.8 = (f32[8,10112]{1,0:T(8,128)}, f32[8,10112]{1,0:T(8,128)S(1)}, u32[]{:S(2)}, u32[]{:S(2)}) collective-permute-start(f32[8,10112]{1,0:T(8,128)} %copy-done), channel_id=1, source_target_pairs={{0,24},{8,0},{16,8},{24,16},{1,25},{9,1},{17,9},{25,17},{2,26},{10... | collective-permute-start | bytes 970760 | tf_op jit(solution)/shard_map/ppermute | solution.py:219
  58.5 1.5 %pad.7.now_ref.prev_ref = f32[25,2,8,896]{3,2,1,0:T(8,128)S(1)} pad(f32[25,2,8,800]{3,2,1,0:T(8,128)} %bitcast.32, f32[]{:T(128)} %constant.27.clone.1), padding=0_0x0_0x0_0x0_96 | pad | bytes 2713604 | tf_op jit(solution)/shard_map/jit(_pad)/pad | solution.py:352
  60.0 3.6 %copy.22 = f32[8,8,25,800]{3,0,1,2:T(8,128)S(1)} copy(f32[8,8,25,800]{3,1,2,0:T(8,128)} %param.10) | data formatting | bytes 10240000 | tf_op args[4]
  65.1 6.1 %wave.4 = (f32[25,2,8,896]{3,2,1,0:T(8,128)S(1)}, f32[4,2,8,896]{3,2,1,0:T(8,128)S(1)}, f32[4,2,8,896]{3,2,1,0:T(8,128)S(1)}) custom-call(s32[2,8]{1,0:T(2,128)S(1)} %pad_add_fusion.source_ref, f32[4,2,8,896]{3,2,1,0:T(8,128)} %collective-permute-done.12.left_ref, f32[4,2,8,896]{3,2,1,0:T(8,128)} %collective-permute-done.13.right_ref, ...), custom_call_target="tpu_custom_call" | custom-call | tf_op jit(solution)/shard_map/wave/pallas_call | solution.py:312
  71.3 4.3 %collective-permute-start.14 = (f32[4,2,8,896]{3,2,1,0:T(8,128)S(1)}, f32[4,2,8,896]{3,2,1,0:T(8,128)S(1)}, u32[]{:S(2)}, u32[]{:S(2)}) collective-permute-start(f32[4,2,8,896]{3,2,1,0:T(8,128)S(1)} %get-tuple-element.40), channel_id=1, source_target_pairs={{0,1},{1,2},{2,3},{3,4},{4,5},{5,6},{6,7},{8,9},{9,10},{10,11},{11... | collective-permute-start | bytes 688136 | tf_op jit(solution)/shard_map/ppermute | solution.py:359
  75.7 1.9 %collective-permute-start.15 = (f32[4,2,8,896]{3,2,1,0:T(8,128)S(1)}, f32[4,2,8,896]{3,2,1,0:T(8,128)S(1)}, u32[]{:S(2)}, u32[]{:S(2)}) collective-permute-start(f32[4,2,8,896]{3,2,1,0:T(8,128)S(1)} %get-tuple-element.41), channel_id=1, source_target_pairs={{1,0},{2,1},{3,2},{4,3},{5,4},{6,5},{7,6},{9,8},{10,9},{11,10},{12... | collective-permute-start | bytes 688136 | tf_op jit(solution)/shard_map/ppermute | solution.py:360
  77.6 2.4 %update.1 = (f32[8,10112]{1,0:T(8,128)S(1)}, f32[8,10112]{1,0:T(8,128)S(1)}, f32[8,10112]{1,0:T(8,128)S(1)}, f32[8,10112]{1,0:T(8,128)S(1)}) custom-call(s32[1]{0:T(128)} %bitcast.me_ref, f32[32,32]{1,0:T(8,128)S(1)} %add_add_fusion.dist_ref, f32[8,10112]{1,0:T(8,128)S(1)} %get-tuple-element.26.refs_0_, f32[8,10112]{1,0:T(8,128)S(1)} %collective-permute-done.refs_1_, ...), custom_call_target="tpu_custom_call" | custom-call | tf_op jit(solution)/shard_map/update/pallas_call | solution.py:206
  81.2 1.9 %collective-permute-start.11 = (f32[8,10112]{1,0:T(8,128)S(1)}, f32[8,10112]{1,0:T(8,128)S(1)}, u32[]{:S(2)}, u32[]{:S(2)}) collective-permute-start(f32[8,10112]{1,0:T(8,128)S(1)} %get-tuple-element.37), channel_id=1, source_target_pairs={{0,24},{8,0},{16,8},{24,16},{1,25},{9,1},{17,9},{25,17},{2,26},{10... | collective-permute-start | bytes 970760 | tf_op jit(solution)/shard_map/ppermute | solution.py:219
  83.6 5.6 %wave.5 = (f32[25,2,8,896]{3,2,1,0:T(8,128)S(1)}, f32[4,2,8,896]{3,2,1,0:T(8,128)S(1)}, f32[4,2,8,896]{3,2,1,0:T(8,128)S(1)}) custom-call(s32[2,8]{1,0:T(2,128)S(1)} %pad_add_fusion.source_ref, f32[4,2,8,896]{3,2,1,0:T(8,128)S(1)} %collective-permute-done.14.left_ref, f32[4,2,8,896]{3,2,1,0:T(8,128)S(1)} %collective-permute-done.15.right_ref, ...), custom_call_target="tpu_custom_call" | custom-call | tf_op jit(solution)/shard_map/wave/pallas_call | solution.py:312
  89.3 4.2 %collective-permute-start.16 = (f32[4,2,8,896]{3,2,1,0:T(8,128)S(1)}, f32[4,2,8,896]{3,2,1,0:T(8,128)S(1)}, u32[]{:S(2)}, u32[]{:S(2)}) collective-permute-start(f32[4,2,8,896]{3,2,1,0:T(8,128)S(1)} %get-tuple-element.43), channel_id=1, source_target_pairs={{0,1},{1,2},{2,3},{3,4},{4,5},{5,6},{6,7},{8,9},{9,10},{10,11},{11... | collective-permute-start | bytes 688136 | tf_op jit(solution)/shard_map/ppermute | solution.py:359
  93.5 1.9 %collective-permute-start.17 = (f32[4,2,8,896]{3,2,1,0:T(8,128)S(1)}, f32[4,2,8,896]{3,2,1,0:T(8,128)S(1)}, u32[]{:S(2)}, u32[]{:S(2)}) collective-permute-start(f32[4,2,8,896]{3,2,1,0:T(8,128)S(1)} %get-tuple-element.44), channel_id=1, source_target_pairs={{1,0},{2,1},{3,2},{4,3},{5,4},{6,5},{7,6},{9,8},{10,9},{11,10},{12... | collective-permute-start | bytes 688136 | tf_op jit(solution)/shard_map/ppermute | solution.py:360
  95.4 7.0 %collective-permute-done.10.refs_2_ = f32[8,10112]{1,0:T(8,128)S(1)} collective-permute-done((f32[8,10112]{1,0:T(8,128)S(1)}, f32[8,10112]{1,0:T(8,128)S(1)}, u32[]{:S(2)}, u32[]{:S(2)}) %collective-permute-start.10) | collective-permute-done | bytes 323616 | tf_op jit(solution)/shard_map/ppermute | solution.py:219
  102.4 7.2 %collective-permute-done.11.refs_3_ = f32[8,10112]{1,0:T(8,128)S(1)} collective-permute-done((f32[8,10112]{1,0:T(8,128)S(1)}, f32[8,10112]{1,0:T(8,128)S(1)}, u32[]{:S(2)}, u32[]{:S(2)}) %collective-permute-start.11) | collective-permute-done | bytes 323616 | tf_op jit(solution)/shard_map/ppermute | solution.py:219
  109.8 1.8 %copy.14 = f32[8,2,25,800]{3,1,2,0:T(2,128)} copy(f32[8,2,25,800]{3,0,1,2:T(8,128)S(1)} %bitcast.29) | data formatting | bytes 2560000
  111.7 5.7 %wave.6 = (f32[25,2,8,896]{3,2,1,0:T(8,128)S(1)}, f32[4,2,8,896]{3,2,1,0:T(8,128)S(1)}, f32[4,2,8,896]{3,2,1,0:T(8,128)S(1)}) custom-call(s32[2,8]{1,0:T(2,128)S(1)} %pad_add_fusion.source_ref, f32[4,2,8,896]{3,2,1,0:T(8,128)S(1)} %collective-permute-done.16.left_ref, f32[4,2,8,896]{3,2,1,0:T(8,128)S(1)} %collective-permute-done.17.right_ref, ...), custom_call_target="tpu_custom_call" | custom-call | tf_op jit(solution)/shard_map/wave/pallas_call | solution.py:312
  117.3 5.3 %collective-permute-start.18 = (f32[4,2,8,896]{3,2,1,0:T(8,128)S(1)}, f32[4,2,8,896]{3,2,1,0:T(8,128)S(1)}, u32[]{:S(2)}, u32[]{:S(2)}) collective-permute-start(f32[4,2,8,896]{3,2,1,0:T(8,128)S(1)} %get-tuple-element.47), channel_id=1, source_target_pairs={{0,1},{1,2},{2,3},{3,4},{4,5},{5,6},{6,7},{8,9},{9,10},{10,11},{11... | collective-permute-start | bytes 688136 | tf_op jit(solution)/shard_map/ppermute | solution.py:359
  122.7 1.9 %collective-permute-start.19 = (f32[4,2,8,896]{3,2,1,0:T(8,128)S(1)}, f32[4,2,8,896]{3,2,1,0:T(8,128)S(1)}, u32[]{:S(2)}, u32[]{:S(2)}) collective-permute-start(f32[4,2,8,896]{3,2,1,0:T(8,128)S(1)} %get-tuple-element.48), channel_id=1, source_target_pairs={{1,0},{2,1},{3,2},{4,3},{5,4},{6,5},{7,6},{9,8},{10,9},{11,10},{12... | collective-permute-start | bytes 688136 | tf_op jit(solution)/shard_map/ppermute | solution.py:360
  124.7 1.8 %copy.15 = f32[8,2,25,800]{3,1,2,0:T(2,128)} copy(f32[8,2,25,800]{3,0,1,2:T(8,128)S(1)} %slice_bitcast_fusion.1) | data formatting | bytes 2560000
  126.6 3.5 %collective-permute-done.19.right_ref = f32[4,2,8,896]{3,2,1,0:T(8,128)S(1)} collective-permute-done((f32[4,2,8,896]{3,2,1,0:T(8,128)S(1)}, f32[4,2,8,896]{3,2,1,0:T(8,128)S(1)}, u32[]{:S(2)}, u32[]{:S(2)}) %collective-permute-start.19) | collective-permute-done | bytes 229408 | tf_op jit(solution)/shard_map/ppermute | solution.py:360
  130.0 5.6 %wave.7 = f32[25,2,8,896]{3,2,1,0:T(8,128)S(1)} custom-call(s32[2,8]{1,0:T(2,128)S(1)} %pad_add_fusion.source_ref, f32[4,2,8,896]{3,2,1,0:T(8,128)S(1)} %collective-permute-done.18.left_ref, f32[4,2,8,896]{3,2,1,0:T(8,128)S(1)} %collective-permute-done.19.right_ref, f32[25,2,8,896]{3,2,1,0:T(8,128)S(1)} %get-tuple-element.46.now_ref, ...), custom_call_target="tpu_custom_call" | custom-call | tf_op jit(solution)/shard_map/wave/pallas_call | solution.py:312
  135.8 1.8 %copy.16 = f32[8,2,25,800]{3,1,2,0:T(2,128)} copy(f32[8,2,25,800]{3,0,1,2:T(8,128)S(1)} %slice_bitcast_fusion) | data formatting | bytes 2560000
  (48 shorter events, 12.6 us)
Async XLA Ops:
  3.1 17.5 %collective-permute-start = (f32[8,10112]{1,0:T(8,128)S(1)}, f32[8,10112]{1,0:T(8,128)S(1)}, u32[]{:S(2)}, u32[]{:S(2)}) collective-permute-start(f32[8,10112]{1,0:T(8,128)S(1)} %get-tuple-element.27), channel_id=1, source_target_pairs={{0,8},{8,16},{16,24},{24,0},{1,9},{9,17},{17,25},{25,1},{2,10},{10... | collective-permute-start | bytes 970760 | tf_op jit(solution)/shard_map/ppermute | solution.py:219
  4.4 28.6 %collective-permute-start.1 = (f32[8,10112]{1,0:T(8,128)}, f32[8,10112]{1,0:T(8,128)S(1)}, u32[]{:S(2)}, u32[]{:S(2)}) collective-permute-start(f32[8,10112]{1,0:T(8,128)} %get-tuple-element.28), channel_id=1, source_target_pairs={{0,16},{8,24},{16,0},{24,8},{1,17},{9,25},{17,1},{25,9},{2,18},{10... | collective-permute-start | bytes 970760 | tf_op jit(solution)/shard_map/ppermute | solution.py:219
  5.4 39.3 %collective-permute-start.2 = (f32[8,10112]{1,0:T(8,128)}, f32[8,10112]{1,0:T(8,128)S(1)}, u32[]{:S(2)}, u32[]{:S(2)}) collective-permute-start(f32[8,10112]{1,0:T(8,128)} %get-tuple-element.29), channel_id=1, source_target_pairs={{0,24},{8,0},{16,8},{24,16},{1,25},{9,1},{17,9},{25,17},{2,26},{10... | collective-permute-start | bytes 970760 | tf_op jit(solution)/shard_map/ppermute | solution.py:219
  8.4 1.1 copy-start.3
  10.3 45.5 %collective-permute-start.12 = (f32[4,2,8,896]{3,2,1,0:T(8,128)}, f32[4,2,8,896]{3,2,1,0:T(8,128)}, u32[]{:S(2)}, u32[]{:S(2)}) collective-permute-start(f32[4,2,8,896]{3,2,1,0:T(8,128)} %get-tuple-element.53), channel_id=1, source_target_pairs={{0,1},{1,2},{2,3},{3,4},{4,5},{5,6},{6,7},{8,9},{9,10},{10,11},{11... | collective-permute-start | bytes 688136 | tf_op jit(solution)/shard_map/ppermute | solution.py:359
  14.8 42.5 %collective-permute-start.13 = (f32[4,2,8,896]{3,2,1,0:T(8,128)}, f32[4,2,8,896]{3,2,1,0:T(8,128)}, u32[]{:S(2)}, u32[]{:S(2)}) collective-permute-start(f32[4,2,8,896]{3,2,1,0:T(8,128)} %get-tuple-element.52), channel_id=1, source_target_pairs={{1,0},{2,1},{3,2},{4,3},{5,4},{6,5},{7,6},{9,8},{10,9},{11,10},{12... | collective-permute-start | bytes 688136 | tf_op jit(solution)/shard_map/ppermute | solution.py:360
  18.2 37.5 %copy-start.5 = (s32[8]{0:T(128)S(1)}, s32[8]{0:T(128)}, u32[]{:S(2)}) copy-start(s32[8]{0:T(128)} %param.11) | copy-start | bytes 100
  18.4 0.7 copy-start
  19.1 0.7 copy-start.1
  19.9 0.7 copy-start.2
  20.6 57.0 %collective-permute-start.6 = (f32[8,10112]{1,0:T(8,128)}, f32[8,10112]{1,0:T(8,128)S(1)}, u32[]{:S(2)}, u32[]{:S(2)}) collective-permute-start(f32[8,10112]{1,0:T(8,128)} %copy-done.2), channel_id=1, source_target_pairs={{0,8},{8,16},{16,24},{24,0},{1,9},{9,17},{17,25},{25,1},{2,10},{10... | collective-permute-start | bytes 970760 | tf_op jit(solution)/shard_map/ppermute | solution.py:219
  33.0 44.6 %collective-permute-start.7 = (f32[8,10112]{1,0:T(8,128)}, f32[8,10112]{1,0:T(8,128)}, u32[]{:S(2)}, u32[]{:S(2)}) collective-permute-start(f32[8,10112]{1,0:T(8,128)} %copy-done.1), channel_id=1, source_target_pairs={{0,16},{8,24},{16,0},{24,8},{1,17},{9,25},{17,1},{25,9},{2,18},{10... | collective-permute-start | bytes 970760 | tf_op jit(solution)/shard_map/ppermute | solution.py:219
  55.7 2.6 %collective-permute-start.3 = (f32[32,32]{1,0:T(8,128)S(1)}, f32[32,32]{1,0:T(8,128)S(1)}, u32[]{:S(2)}, u32[]{:S(2)}) collective-permute-start(f32[32,32]{1,0:T(8,128)S(1)} %reduce_sum.9), channel_id=1, source_target_pairs={{0,8},{8,16},{16,24},{24,0},{1,9},{9,17},{17,25},{25,1},{2,10},{10... | collective-permute-start | bytes 12296 | tf_op jit(solution)/shard_map/ppermute | solution.py:219
  55.8 21.8 %collective-permute-start.8 = (f32[8,10112]{1,0:T(8,128)}, f32[8,10112]{1,0:T(8,128)S(1)}, u32[]{:S(2)}, u32[]{:S(2)}) collective-permute-start(f32[8,10112]{1,0:T(8,128)} %copy-done), channel_id=1, source_target_pairs={{0,24},{8,0},{16,8},{24,16},{1,25},{9,1},{17,9},{25,17},{2,26},{10... | collective-permute-start | bytes 970760 | tf_op jit(solution)/shard_map/ppermute | solution.py:219
  57.3 14.0 %collective-permute-start.4 = (f32[32,32]{1,0:T(8,128)S(1)}, f32[32,32]{1,0:T(8,128)S(1)}, u32[]{:S(2)}, u32[]{:S(2)}) collective-permute-start(f32[32,32]{1,0:T(8,128)S(1)} %reduce_sum.9), channel_id=1, source_target_pairs={{0,16},{8,24},{16,0},{24,8},{1,17},{9,25},{17,1},{25,9},{2,18},{10... | collective-permute-start | bytes 12296 | tf_op jit(solution)/shard_map/ppermute | solution.py:219
  58.3 17.3 %collective-permute-start.5 = (f32[32,32]{1,0:T(8,128)S(1)}, f32[32,32]{1,0:T(8,128)S(1)}, u32[]{:S(2)}, u32[]{:S(2)}) collective-permute-start(f32[32,32]{1,0:T(8,128)S(1)} %reduce_sum.9), channel_id=1, source_target_pairs={{0,24},{8,0},{16,8},{24,16},{1,25},{9,1},{17,9},{25,17},{2,26},{10... | collective-permute-start | bytes 12296 | tf_op jit(solution)/shard_map/ppermute | solution.py:219
  63.6 1.4 copy-start.4
  71.3 12.3 %collective-permute-start.14 = (f32[4,2,8,896]{3,2,1,0:T(8,128)S(1)}, f32[4,2,8,896]{3,2,1,0:T(8,128)S(1)}, u32[]{:S(2)}, u32[]{:S(2)}) collective-permute-start(f32[4,2,8,896]{3,2,1,0:T(8,128)S(1)} %get-tuple-element.40), channel_id=1, source_target_pairs={{0,1},{1,2},{2,3},{3,4},{4,5},{5,6},{6,7},{8,9},{9,10},{10,11},{11... | collective-permute-start | bytes 688136 | tf_op jit(solution)/shard_map/ppermute | solution.py:359
  75.7 8.0 %collective-permute-start.15 = (f32[4,2,8,896]{3,2,1,0:T(8,128)S(1)}, f32[4,2,8,896]{3,2,1,0:T(8,128)S(1)}, u32[]{:S(2)}, u32[]{:S(2)}) collective-permute-start(f32[4,2,8,896]{3,2,1,0:T(8,128)S(1)} %get-tuple-element.41), channel_id=1, source_target_pairs={{1,0},{2,1},{3,2},{4,3},{5,4},{6,5},{7,6},{9,8},{10,9},{11,10},{12... | collective-permute-start | bytes 688136 | tf_op jit(solution)/shard_map/ppermute | solution.py:360
  80.1 22.3 %collective-permute-start.10 = (f32[8,10112]{1,0:T(8,128)S(1)}, f32[8,10112]{1,0:T(8,128)S(1)}, u32[]{:S(2)}, u32[]{:S(2)}) collective-permute-start(f32[8,10112]{1,0:T(8,128)S(1)} %get-tuple-element.36), channel_id=1, source_target_pairs={{0,16},{8,24},{16,0},{24,8},{1,17},{9,25},{17,1},{25,9},{2,18},{10... | collective-permute-start | bytes 970760 | tf_op jit(solution)/shard_map/ppermute | solution.py:219
  81.2 28.4 %collective-permute-start.11 = (f32[8,10112]{1,0:T(8,128)S(1)}, f32[8,10112]{1,0:T(8,128)S(1)}, u32[]{:S(2)}, u32[]{:S(2)}) collective-permute-start(f32[8,10112]{1,0:T(8,128)S(1)} %get-tuple-element.37), channel_id=1, source_target_pairs={{0,24},{8,0},{16,8},{24,16},{1,25},{9,1},{17,9},{25,17},{2,26},{10... | collective-permute-start | bytes 970760 | tf_op jit(solution)/shard_map/ppermute | solution.py:219
  83.1 26.5 %collective-permute-start.9 = (f32[8,10112]{1,0:T(8,128)S(1)}, f32[8,10112]{1,0:T(8,128)S(1)}, u32[]{:S(2)}, u32[]{:S(2)}) collective-permute-start(f32[8,10112]{1,0:T(8,128)S(1)} %get-tuple-element.35), channel_id=1, source_target_pairs={{0,8},{8,16},{16,24},{24,0},{1,9},{9,17},{17,25},{25,1},{2,10},{10... | collective-permute-start | bytes 970760 | tf_op jit(solution)/shard_map/ppermute | solution.py:219
  89.3 22.4 %collective-permute-start.16 = (f32[4,2,8,896]{3,2,1,0:T(8,128)S(1)}, f32[4,2,8,896]{3,2,1,0:T(8,128)S(1)}, u32[]{:S(2)}, u32[]{:S(2)}) collective-permute-start(f32[4,2,8,896]{3,2,1,0:T(8,128)S(1)} %get-tuple-element.43), channel_id=1, source_target_pairs={{0,1},{1,2},{2,3},{3,4},{4,5},{5,6},{6,7},{8,9},{9,10},{10,11},{11... | collective-permute-start | bytes 688136 | tf_op jit(solution)/shard_map/ppermute | solution.py:359
  93.5 18.2 %collective-permute-start.17 = (f32[4,2,8,896]{3,2,1,0:T(8,128)S(1)}, f32[4,2,8,896]{3,2,1,0:T(8,128)S(1)}, u32[]{:S(2)}, u32[]{:S(2)}) collective-permute-start(f32[4,2,8,896]{3,2,1,0:T(8,128)S(1)} %get-tuple-element.44), channel_id=1, source_target_pairs={{1,0},{2,1},{3,2},{4,3},{5,4},{6,5},{7,6},{9,8},{10,9},{11,10},{12... | collective-permute-start | bytes 688136 | tf_op jit(solution)/shard_map/ppermute | solution.py:360
  117.3 9.2 %collective-permute-start.18 = (f32[4,2,8,896]{3,2,1,0:T(8,128)S(1)}, f32[4,2,8,896]{3,2,1,0:T(8,128)S(1)}, u32[]{:S(2)}, u32[]{:S(2)}) collective-permute-start(f32[4,2,8,896]{3,2,1,0:T(8,128)S(1)} %get-tuple-element.47), channel_id=1, source_target_pairs={{0,1},{1,2},{2,3},{3,4},{4,5},{5,6},{6,7},{8,9},{9,10},{10,11},{11... | collective-permute-start | bytes 688136 | tf_op jit(solution)/shard_map/ppermute | solution.py:359
  122.7 7.3 %collective-permute-start.19 = (f32[4,2,8,896]{3,2,1,0:T(8,128)S(1)}, f32[4,2,8,896]{3,2,1,0:T(8,128)S(1)}, u32[]{:S(2)}, u32[]{:S(2)}) collective-permute-start(f32[4,2,8,896]{3,2,1,0:T(8,128)S(1)} %get-tuple-element.48), channel_id=1, source_target_pairs={{1,0},{2,1},{3,2},{4,3},{5,4},{6,5},{7,6},{9,8},{10,9},{11,10},{12... | collective-permute-start | bytes 688136 | tf_op jit(solution)/shard_map/ppermute | solution.py:360
